TPU v7x, 128 devices: a whole 4x4x4 slice. The times are simulated.
128 devices in a mesh: ctx: 64 (over z, y, x), head: 2 (over core).
Axes of the slice: x: 4, y: 4, z: 4, core: 2. Of those that a mesh axis runs over, the one named last changes fastest.
Arguments:
- query: bfloat16 [24576, 6144], P(('ctx', 'head')), may hold values from -6 to 6
- key_in: bfloat16 [24576, 6144], P(('ctx', 'head')), may hold values from -6 to 6
- value: bfloat16 [24576, 6144], P(('ctx', 'head')), may hold values from -6 to 6
- cotangent: bfloat16 [24576, 6144], P(('ctx', 'head')), may hold values from -18 to 18
- decay_rate: float32 [48, 16], replicated, as said below
- residue: float32 [48, 16], replicated, may hold values from -2 to 2
Outputs:
- mixed: bfloat16 [24576, 6144], P(('ctx', 'head'))
- grad_query: bfloat16 [24576, 6144], P(('ctx', 'head'))
- grad_key: bfloat16 [24576, 6144], P(('ctx', 'head'))
- grad_value: bfloat16 [24576, 6144], P(('ctx', 'head'))
- residue_grad: float32 [48, 16], P('head')
Inputs may be any that keep to these rules, and one draw needn't show every extreme that they name: `decay_rate`: positive decay rates of at most 1/30.
All inputs are finite; a program needn't handle non-finite values.
Results may differ from a plain program's by a relative error of at most 0.00105.
Values may be sent and summed in bfloat16 or wider, within the bound.
No kernel may reach another device: no remote copies, remote signals or barrier semaphores. Data moves between devices by JAX's collectives and lax.ppermute only.
A program may use at most 192 MiB of HBM per device.

v0:
```python
import math
import jax
import jax.numpy as jnp
from jax import lax
from jax.sharding import PartitionSpec as P

HEAD_DIM = 128
SPAN = 768
HIGHEST = lax.Precision.HIGHEST


def entering_2(part, axis, combine, identity, reverse):
    count = lax.axis_size(axis)
    place = lax.axis_index(axis)
    ahead = count - 1 - place if reverse else place
    gathered = jax.tree.map(lambda a: lax.all_gather(a, axis), part)
    state = jax.tree.map(lambda a, e: jnp.zeros_like(a) + jnp.asarray(e, a.dtype), part, identity)

    def one(lap, state):
        source = count - 1 - lap if reverse else lap
        return combine(
            state, jax.tree.map(lambda a: lax.dynamic_index_in_dim(a, source, 0, False), gathered)
        )

    return lax.fori_loop(0, ahead, one, state)


def combine_states(earlier, later_part):
    return (earlier[0] * later_part[0], later_part[0][..., None] * earlier[1] + later_part[1])


def modal_layer(
    query,
    key_in,
    value,
    cotangent,
    decay_rate,
    residue,
    block_rows,
    forward_chain,
    backward_chain,
    seq_total,
):
    row_count, feature_count = query.shape
    head_count = decay_rate.shape[0]
    head_size = feature_count // head_count
    block_count = row_count // block_rows

    def blocked(source):
        return source.reshape(block_count, block_rows, head_count, head_size).astype(jnp.float32)

    query_wide = blocked(query)
    key_wide = blocked(key_in)
    value_wide = blocked(value)
    cotan_wide = blocked(cotangent)
    product = key_wide * value_wide
    norm_factor = jnp.sqrt(-jnp.expm1(-2.0 * decay_rate))
    coefficient = residue * norm_factor
    offsets = jnp.arange(block_rows, dtype=jnp.float32)
    decay_in = jnp.exp(-decay_rate[:, :, None] * offsets)
    decay_end = jnp.exp(-decay_rate[:, :, None] * (float(block_rows - 1) - offsets))
    growth = jnp.exp(decay_rate[:, :, None] * offsets)
    one_step = jnp.exp(-decay_rate)
    lag_index = lax.broadcasted_iota(jnp.int32, (block_rows, block_rows), 0) - lax.broadcasted_iota(
        jnp.int32, (block_rows, block_rows), 1
    )
    lower = lag_index[None] >= 0
    weighted_in = coefficient[:, :, None] * decay_in
    full_table = jnp.einsum("hmi,hmj->hij", weighted_in, growth, precision=HIGHEST)
    toeplitz = jnp.where(lower, full_table, 0.0)
    inner_part = jnp.einsum("hij,bjhc->bihc", toeplitz, product, precision=HIGHEST)
    block_ends = jnp.einsum("hmj,bjhc->bhmc", decay_end, product, precision=HIGHEST)
    block_decay = jnp.exp(-decay_rate * block_rows)[:, :, None]

    def walk_forward(state, block_end):
        return (block_decay * state + block_end, state)

    zero_state = jnp.zeros(block_ends.shape[1:], jnp.float32)
    device_total, entering_local = lax.scan(walk_forward, zero_state, block_ends)
    device_decay = jnp.exp(-decay_rate * row_count)
    incoming = forward_chain(device_decay, device_total)
    block_starts = jnp.arange(block_count, dtype=jnp.float32) * block_rows
    block_powers = jnp.exp(-decay_rate[None] * block_starts[:, None, None])[..., None]
    later_starts = (
        float(block_count - 1) - jnp.arange(block_count, dtype=jnp.float32)
    ) * block_rows
    later_powers = jnp.exp(-decay_rate[None] * later_starts[:, None, None])[..., None]
    entering = entering_local + block_powers * incoming[None]
    inflow = coefficient[:, :, None] * one_step[:, :, None] * decay_in
    outer_part = jnp.einsum("hmi,bhmc->bihc", inflow, entering, precision=HIGHEST)
    convolved = inner_part + outer_part
    mixed = (query_wide * convolved).reshape(row_count, feature_count).astype(jnp.bfloat16)
    grad_conv = cotan_wide * query_wide
    grad_query = (cotan_wide * convolved).reshape(row_count, feature_count).astype(jnp.bfloat16)
    back_inner = jnp.einsum("hij,bihc->bjhc", toeplitz, grad_conv, precision=HIGHEST)
    block_heads = jnp.einsum("hmi,bihc->bhmc", decay_in, grad_conv, precision=HIGHEST)

    def walk_backward(state, block_head):
        return (block_decay * state + block_head, state)

    back_total, later_local = lax.scan(walk_backward, zero_state, block_heads, reverse=True)
    outgoing = backward_chain(device_decay, back_total)
    later_states = later_local + later_powers * outgoing[None]
    outflow = coefficient[:, :, None] * one_step[:, :, None] * decay_end
    back_outer = jnp.einsum("hmj,bhmc->bjhc", outflow, later_states, precision=HIGHEST)
    grad_product = back_inner + back_outer
    grad_key = (grad_product * value_wide).reshape(row_count, feature_count).astype(jnp.bfloat16)
    grad_value = (grad_product * key_wide).reshape(row_count, feature_count).astype(jnp.bfloat16)
    cross_table = jnp.einsum("bihc,bjhc->hij", grad_conv, product, precision=HIGHEST)
    cross_lower = jnp.where(lower, cross_table, 0.0)
    grown_rows = jnp.einsum("hij,hmj->hmi", cross_lower, growth, precision=HIGHEST)
    near_terms = jnp.sum(grown_rows * decay_in, axis=2)
    far_terms = one_step * jnp.einsum("bhmc,bhmc->hm", block_heads, entering, precision=HIGHEST)
    residue_terms = norm_factor * (near_terms + far_terms) / math.sqrt(float(seq_total * HEAD_DIM))
    return (mixed, grad_query, grad_key, grad_value, residue_terms)


def on_device(query, key_in, value, cotangent, decay_rate, residue):
    seq_total = query.shape[0] * lax.axis_size("ctx") * lax.axis_size("head")
    group_heads = decay_rate.shape[0] // lax.axis_size("head")
    first_head = lax.axis_index("head") * group_heads
    local_rates = lax.dynamic_slice_in_dim(decay_rate, first_head, group_heads, 0)
    local_residue = lax.dynamic_slice_in_dim(residue, first_head, group_heads, 0)
    arrived = (
        lax.all_to_all(query, "head", split_axis=1, concat_axis=0, tiled=True),
        lax.all_to_all(key_in, "head", split_axis=1, concat_axis=0, tiled=True),
        lax.all_to_all(value, "head", split_axis=1, concat_axis=0, tiled=True),
        lax.all_to_all(cotangent, "head", split_axis=1, concat_axis=0, tiled=True),
    )
    block_rows = min(SPAN, arrived[0].shape[0])

    def forward_chain(decays, totals):
        return entering_2(
            (decays, totals),
            "ctx",
            combine_states,
            (jnp.ones_like(decays), jnp.zeros_like(totals)),
            False,
        )[1]

    def backward_chain(decays, totals):
        return entering_2(
            (decays, totals),
            "ctx",
            combine_states,
            (jnp.ones_like(decays), jnp.zeros_like(totals)),
            True,
        )[1]

    results = modal_layer(
        arrived[0],
        arrived[1],
        arrived[2],
        arrived[3],
        local_rates,
        local_residue,
        block_rows,
        forward_chain,
        backward_chain,
        seq_total,
    )
    returned = (
        lax.all_to_all(results[0], "head", split_axis=0, concat_axis=1, tiled=True),
        lax.all_to_all(results[1], "head", split_axis=0, concat_axis=1, tiled=True),
        lax.all_to_all(results[2], "head", split_axis=0, concat_axis=1, tiled=True),
        lax.all_to_all(results[3], "head", split_axis=0, concat_axis=1, tiled=True),
    )
    residue_grad = lax.psum(results[4], "ctx")
    return (returned[0], returned[1], returned[2], returned[3], residue_grad)


def solution(mesh):
    placed = (
        P(("ctx", "head"), None),
        P(("ctx", "head"), None),
        P(("ctx", "head"), None),
        P(("ctx", "head"), None),
        P(),
        P(),
    )
    return jax.shard_map(
        on_device,
        mesh=mesh,
        in_specs=placed,
        out_specs=(
            P(("ctx", "head"), None),
            P(("ctx", "head"), None),
            P(("ctx", "head"), None),
            P(("ctx", "head"), None),
            P("head", None),
        ),
        check_vma=False,
    )
```

profile of v0, /device:TPU:1, one launch (start us, length us, event | category | flops | bytes accessed | tf_op | source)
XLA Modules:
  0.0 1042.2 jit_solution(16150171669965274029)
XLA Ops:
  7.2 3.3 copy.159
  10.4 5.2 all-to-all-start.2
  15.8 3.2 copy.160
  19.1 6.6 all_to_all.116
  28.0 2.1 copy-done
  30.1 4.2 fusion.37
  34.3 3.2 copy.158
  37.6 5.3 all-to-all-start.4
  42.8 3.2 copy.161
  46.1 6.6 all_to_all.117
  52.7 3.4 convert_multiply_fusion
  56.1 3.1 copy.131
  59.2 155.4 %all-gather.1 = f32[64,24,16]{1,2,0:T(8,128)S(1)} all-gather(f32[1,24,16]{1,2,0:T(8,128)S(1)} %copy.92), channel_id=2, replica_groups=mesh['ctx'=64,'head'=2] {'ctx'}, dimensions={0}, use_global_device_ids=true | all-gather | bytes 99840 | tf_op jit(solution)/shard_map/all_gather | solution.py:16
  214.7 1.2 copy.94
  215.9 11.2 %while.16 = (s32[]{:T(128)}, f32[24,16,128]{2,1,0:T(8,128)S(1)}, s32[]{:T(128)}, f32[64,24,16]{2,1,0:T(8,128)}, f32[64,24,16,128]{3,2,1,0:T(8,128)}, /*index=5*/s32[]{:T(128)}, s32[]{:T(128)}, s32[]{:T(128)}) while((s32[]{:T(128)}, f32[24,16,128]{2,1,0:T(8,128)S(1)}, s32[]{:T(128)}, f32[64,24,16]{2,1,0:T(8,128)}, ...), condition=%wide.region_1.2_spmd, body=%wide.region_0.1_spmd.sunk | while | flops 98309 | bytes 594567 | solution.py:25
  227.1 5.9 fusion.56
  233.8 2.2 convert_element_type.157
  236.0 3.2 copy.130
  239.2 6.1 copy.99
  245.3 2.2 convert_element_type.156
  247.5 3.2 copy.128
  250.7 6.1 copy.95
  256.9 2.2 convert_element_type.131
  259.1 3.1 copy.133
  262.2 6.0 copy.108
  268.8 3.1 copy.132
  271.9 6.1 copy.105
  278.0 15.8 %fusion.17 = f32[24,384,384]{2,1,0:T(8,128)S(1)} fusion(f32[384,24,128]{2,1,0:T(8,128)} %bitcast.123, f32[384,24,128]{2,1,0:T(8,128)} %bitcast.118), kind=kOutput, calls=%fused_computation.25 | convolution fusion | flops 5435817984 | bytes 23592960 | tf_op jit(solution)/shard_map/bihc,bjhc->hij/dot_general | solution.py:109
  293.9 13.5 %fusion.28 = f32[24,16]{1,0:T(8,128)S(1)} fusion(f32[24,384,384]{2,1,0:T(8,128)S(1)} %fusion.17, pred[384,384]{1,0:T(8,128)(4,1)S(1)} %subtract_compare_fusion, f32[24,16]{1,0:T(8,128)S(1)} %copy.119, f32[24,16]{1,0:T(8,128)S(1)} %get-tuple-element.240), kind=kOutput, calls=%fused_computation.42 | convolution fusion | flops 683605632 | bytes 14307840 | tf_op jit(solution)/shard_map/hij,hmj->hmi/dot_general | solution.py:111
  307.4 14.3 %fusion.42 = f32[24,384,384]{2,1,0:T(8,128)} fusion(f32[24,16]{1,0:T(8,128)S(1)} %copy.119, f32[24,16]{1,0:T(8,128)S(1)} %get-tuple-element.240, f32[24,16]{1,0:T(8,128)S(1)} %get-tuple-element.231), kind=kOutput, calls=%fused_computation.50 | convolution fusion | flops 679919616 | bytes 14160384 | tf_op jit(solution)/shard_map/hmi,hmj->hij/dot_general | solution.py:69
  321.8 23.5 %fusion.4 = f32[24,128,384]{2,1,0:T(8,128)} fusion(f32[24,384,384]{2,1,0:T(8,128)} %fusion.42, pred[384,384]{1,0:T(8,128)(4,1)S(1)} %subtract_compare_fusion, f32[384,24,128]{2,1,0:T(8,128)S(1)} %bitcast.121), kind=kOutput, calls=%fused_computation.8 | convolution fusion | flops 5439356928 | bytes 23740416 | tf_op jit(solution)/shard_map/hij,bjhc->bihc/dot_general | solution.py:71
  345.3 9.6 fusion.15
  354.9 3.1 copy.96
  358.0 2.4 convert_element_type.134
  360.4 34.3 %all_to_all.118 = bf16[2,192,3072]{2,1,0:T(8,128)(2,1)S(1)} all-to-all(bf16[2,192,3072]{2,1,0:T(8,128)(2,1)} %convert_element_type.134), channel_id=1, replica_groups=mesh['ctx'=64,'head'=2] {'head'}, dimensions={0} | all-to-all | bytes 4718592 | tf_op jit(solution)/shard_map/all_to_all | solution.py:163
  394.7 1.6 copy.124
  396.3 3.1 copy.100
  399.4 2.4 convert_element_type.139
  401.8 6.9 all_to_all.119
  408.7 1.6 copy.125
  410.3 398.9 %psum.7 = f32[24,16]{1,0:T(8,128)S(1)} all-reduce(f32[24,16]{1,0:T(8,128)S(1)} %get-tuple-element.236), channel_id=1, replica_groups=mesh['ctx'=64,'head'=2] {'ctx'}, use_global_device_ids=true, to_apply=%region_5.6 | all-reduce | flops 384 | bytes 3072 | tf_op jit(solution)/shard_map/psum | solution.py:168
  809.9 19.5 %fusion.2 = f32[24,128,384]{2,1,0:T(8,128)} fusion(f32[24,384,384]{2,1,0:T(8,128)} %fusion.42, pred[384,384]{1,0:T(8,128)(4,1)S(1)} %subtract_compare_fusion, f32[384,24,128]{2,1,0:T(8,128)} %bitcast.124), kind=kOutput, calls=%fused_computation.6 | convolution fusion | flops 5439356928 | bytes 23740416 | tf_op jit(solution)/shard_map/hij,bihc->bjhc/dot_general | solution.py:95
  829.5 112.8 %while.17 = (s32[]{:T(128)}, f32[24,16,128]{2,1,0:T(8,128)S(1)}, s32[]{:T(128)}, f32[64,24,16]{2,1,0:T(8,128)}, f32[64,24,16,128]{3,2,1,0:T(8,128)}, /*index=5*/s32[]{:T(128)}, s32[]{:T(128)}, s32[]{:T(128)}, s32[]{:T(128)}) while((s32[]{:T(128)}, f32[24,16,128]{2,1,0:T(8,128)S(1)}, s32[]{:T(128)}, f32[64,24,16]{2,1,0:T(8,128)}, ...), condition=%wide.region_3.4_spmd, body=%wide.region_2.3_spmd.sunk | while | flops 98310 | bytes 594587 | solution.py:25
  830.2 1.0 bitcast_add_fusion.6
  833.8 1.0 bitcast_add_fusion.6
  835.6 1.0 bitcast_add_fusion.6
  839.1 1.0 bitcast_add_fusion.6
  840.9 1.0 bitcast_add_fusion.6
  842.7 1.0 bitcast_add_fusion.6
  846.3 1.0 bitcast_add_fusion.6
  848.1 1.0 bitcast_add_fusion.6
  851.7 1.0 bitcast_add_fusion.6
  853.5 1.0 bitcast_add_fusion.6
  857.0 1.0 bitcast_add_fusion.6
  858.8 1.0 bitcast_add_fusion.6
  942.3 9.6 fusion.13
  951.9 3.1 copy.106
  955.0 2.4 convert_element_type.146
  957.4 62.1 %all_to_all.120 = bf16[2,192,3072]{2,1,0:T(8,128)(2,1)S(1)} all-to-all(bf16[2,192,3072]{2,1,0:T(8,128)(2,1)} %convert_element_type.146), channel_id=1, replica_groups=mesh['ctx'=64,'head'=2] {'head'}, dimensions={0} | all-to-all | bytes 4718592 | tf_op jit(solution)/shard_map/all_to_all | solution.py:165
  1019.5 1.6 copy.126
  1021.1 3.1 copy.109
  1024.2 2.4 convert_element_type.151
  1026.6 6.8 all_to_all.121
  1033.5 1.6 copy.127
  (151 shorter events, 103.3 us)
Async XLA Ops:
  7.2 8.5 copy-start.3
  7.2 8.5 copy-start.4
  10.4 8.6 all-to-all-start.2
  15.6 200.3 %all-gather.5.cloned.1.call-start = ((), (), s32[]{:S(2)}) async-start(), calls=%async_computation.8 | async-start | bytes 12779520 | tf_op jit(solution)/shard_map/all_gather | solution.py:16
  25.6 1.4 copy-start.1
  28.0 2.1 copy-start
  37.6 8.5 all-to-all-start.4
  42.8 786.6 %all-gather.7.cloned.1.call-start = ((), (), s32[]{:S(2)}) async-start(), calls=%async_computation.9 | async-start | bytes 12779520 | tf_op jit(solution)/shard_map/all_gather | solution.py:16
  52.7 3.4 copy-start.2
  293.9 27.9 %slice-start = ((s8[4718592]{0:T(1024)(128)(4,1)}), s8[4194304]{0:T(1024)(128)(4,1)S(1)}, s32[]{:S(2)}) async-start(s8[4718592]{0:T(1024)(128)(4,1)} %bitcast.119), calls=%async_computation.10 | async-start | bytes 8388608
  307.4 14.4 %slice-start.1 = ((s8[4718592]{0:T(1024)(128)(4,1)}), s8[524288]{0:T(1024)(128)(4,1)S(1)}, s32[]{:S(2)}) async-start(s8[4718592]{0:T(1024)(128)(4,1)} %bitcast.119), calls=%async_computation.11 | async-start | bytes 1048576
Sparse Core Ops, SparseCore 0:
  34.5 94.2 all-gather.4
  233.9 224.1 all-gather.6
where the time goes:
time: 1050 us; the launch traced here: 1040 us
  blocking collectives  678 us (65%)
  local copies, waits for them, and re-layouts  132 us (13%)
  matrix products  116 us (11%)
  other arithmetic  78.4 us (7%)
  between operations  14.5 us (1%)
  loops' own time  13 us (1%)
    psum x1, blocking collectives, on_device(): residue_grad = lax.psum(results[4], 'ctx')  399 us
    all_gather x1, blocking collectives, entering_2(): gathered = jax.tree.map(lambda a: lax.all_gather(a, axis), part)  155 us
    add x63, other arithmetic, combine_states(): later_part[0][..., None] * earlier[1] + later_part[1]  66.1 us
    all_to_all x1, blocking collectives, on_device(): lax.all_to_all(results[2], 'head', split_axis=0, concat_axis=1, tiled=True)  62.1 us
    mul x63, local copies, waits for them, and re-layouts, combine_states(): later_part[0][..., None] * earlier[1] + later_part[1]  44.9 us
    all_to_all x1, blocking collectives, on_device(): lax.all_to_all(results[0], 'head', split_axis=0, concat_axis=1, tiled=True)  34.3 us
    convert_element_type x4, local copies, waits for them, and re-layouts, blocked(): source.reshape(block_count, block_rows, head_count, head_size)  24.3 us
    dot_general x1, matrix products, modal_layer(): jnp.einsum('hij,bjhc->bihc', toeplitz, product, precision=HIGHEST)  23.5 us
  transfers between devices with their start and end apart: 4, of which 0 were waited for; matrix products, arithmetic and copies ran while one was open for 17% of the time, Pallas kernels for 0%

commit v1 on v0

--- a/solution.py
+++ b/solution.py
@@ -165,7 +165,9 @@
         lax.all_to_all(results[2], "head", split_axis=0, concat_axis=1, tiled=True),
         lax.all_to_all(results[3], "head", split_axis=0, concat_axis=1, tiled=True),
     )
-    residue_grad = lax.psum(results[4], "ctx")
+    x = results[4]
+    shards = lax.all_gather(x, "ctx")
+    residue_grad = jnp.sum(shards, axis=0)
     return (returned[0], returned[1], returned[2], returned[3], residue_grad)
 
 

time: 1050 us -> 886 us (0.84)
  blocking collectives: 678 us -> 508 us
    psum x1 -> x0, blocking collectives: 399 us -> none  [on_device(): residue_grad = lax.psum(results[4], 'ctx')]
    all_gather x0 -> x1, blocking collectives: none -> 257 us  [on_device(): shards = lax.all_gather(x, 'ctx')]
    all_to_all x1, blocking collectives: 62.1 us -> 35 us  [on_device(): lax.all_to_all(results[2], 'head', split_axis=0, concat_axis=1, tiled=True)]
  transfers between devices with their start and end apart: 4 -> 4, of which waited for: 0 -> 0; matrix products, arithmetic and copies ran while one was open for 17% -> 20% of each run, Pallas kernels for 0% -> 0%
where the time goes in v1:
time: 886 us; the launch traced here: 873 us
  blocking collectives  508 us (57%)
  local copies, waits for them, and re-layouts  132 us (15%)
  matrix products  116 us (13%)
  other arithmetic  79.1 us (9%)
  between operations  14.5 us (2%)
  loops' own time  13 us (1%)
  starting transfers between devices  10.4 us (1%)
    all_gather x1, blocking collectives, on_device(): shards = lax.all_gather(x, 'ctx')  257 us
    all_gather x1, blocking collectives, entering_2(): gathered = jax.tree.map(lambda a: lax.all_gather(a, axis), part)  155 us
    add x63, other arithmetic, combine_states(): later_part[0][..., None] * earlier[1] + later_part[1]  66.1 us
    mul x63, local copies, waits for them, and re-layouts, combine_states(): later_part[0][..., None] * earlier[1] + later_part[1]  44.9 us
    all_to_all x1, blocking collectives, on_device(): lax.all_to_all(results[2], 'head', split_axis=0, concat_axis=1, tiled=True)  35 us
    all_to_all x1, blocking collectives, on_device(): lax.all_to_all(results[0], 'head', split_axis=0, concat_axis=1, tiled=True)  34.3 us
    convert_element_type x4, local copies, waits for them, and re-layouts, blocked(): source.reshape(block_count, block_rows, head_count, head_size)  24.3 us
    dot_general x1, matrix products, modal_layer(): jnp.einsum('hij,bjhc->bihc', toeplitz, product, precision=HIGHEST)  23.5 us
  transfers between devices with their start and end apart: 4, of which 0 were waited for; matrix products, arithmetic and copies ran while one was open for 20% of the time, Pallas kernels for 0%

profile of v1, /device:TPU:1, one launch (start us, length us, event | category | flops | bytes accessed | tf_op | source)
XLA Modules:
  0.0 872.7 jit_solution(5716490613937317399)
XLA Ops:
  7.2 3.3 copy.174
  10.4 5.2 all-to-all-start.2
  15.8 3.2 copy.175
  19.1 6.6 all_to_all.116
  28.0 2.1 copy-done
  30.1 4.2 fusion.37
  34.3 3.2 copy.173
  37.6 5.3 all-to-all-start.4
  42.8 3.2 copy.176
  46.1 6.6 all_to_all.117
  52.7 3.4 convert_multiply_fusion
  56.1 3.1 copy.146
  59.2 155.4 %all-gather.2 = f32[64,24,16]{1,2,0:T(8,128)S(1)} all-gather(f32[1,24,16]{1,2,0:T(8,128)S(1)} %copy.104), channel_id=2, replica_groups=mesh['ctx'=64,'head'=2] {'ctx'}, dimensions={0}, use_global_device_ids=true | all-gather | bytes 99840 | tf_op jit(solution)/shard_map/all_gather | solution.py:16
  214.7 1.2 copy.106
  215.9 11.2 %while.16 = (s32[]{:T(128)}, f32[24,16,128]{2,1,0:T(8,128)S(1)}, s32[]{:T(128)}, f32[64,24,16]{2,1,0:T(8,128)}, f32[64,24,16,128]{3,2,1,0:T(8,128)}, /*index=5*/s32[]{:T(128)}, s32[]{:T(128)}, s32[]{:T(128)}) while((s32[]{:T(128)}, f32[24,16,128]{2,1,0:T(8,128)S(1)}, s32[]{:T(128)}, f32[64,24,16]{2,1,0:T(8,128)}, ...), condition=%wide.region_1.2_spmd, body=%wide.region_0.1_spmd.sunk | while | flops 98309 | bytes 594567 | solution.py:25
  227.1 5.9 fusion.56
  233.8 2.2 convert_element_type.157
  236.0 3.2 copy.145
  239.2 6.1 copy.111
  245.3 2.2 convert_element_type.156
  247.5 3.2 copy.143
  250.7 6.1 copy.107
  256.9 2.2 convert_element_type.131
  259.1 3.1 copy.148
  262.2 6.0 copy.120
  268.8 3.1 copy.147
  271.9 6.1 copy.117
  278.0 15.8 %fusion.17 = f32[24,384,384]{2,1,0:T(8,128)S(1)} fusion(f32[384,24,128]{2,1,0:T(8,128)} %bitcast.120, f32[384,24,128]{2,1,0:T(8,128)} %bitcast.123), kind=kOutput, calls=%fused_computation.25 | convolution fusion | flops 5435817984 | bytes 23592960 | tf_op jit(solution)/shard_map/bihc,bjhc->hij/dot_general | solution.py:109
  293.9 13.5 %fusion.28 = f32[24,16]{1,0:T(8,128)S(1)} fusion(f32[24,384,384]{2,1,0:T(8,128)S(1)} %fusion.17, pred[384,384]{1,0:T(8,128)(4,1)S(1)} %subtract_compare_fusion, f32[24,16]{1,0:T(8,128)S(1)} %copy.133, f32[24,16]{1,0:T(8,128)S(1)} %get-tuple-element.225), kind=kOutput, calls=%fused_computation.42 | convolution fusion | flops 683605632 | bytes 14307840 | tf_op jit(solution)/shard_map/hij,hmj->hmi/dot_general | solution.py:111
  307.4 14.3 %fusion.42 = f32[24,384,384]{2,1,0:T(8,128)} fusion(f32[24,16]{1,0:T(8,128)S(1)} %copy.133, f32[24,16]{1,0:T(8,128)S(1)} %get-tuple-element.225, f32[24,16]{1,0:T(8,128)S(1)} %get-tuple-element.216), kind=kOutput, calls=%fused_computation.50 | convolution fusion | flops 679919616 | bytes 14160384 | tf_op jit(solution)/shard_map/hmi,hmj->hij/dot_general | solution.py:69
  321.8 23.5 %fusion.4 = f32[24,128,384]{2,1,0:T(8,128)} fusion(f32[24,384,384]{2,1,0:T(8,128)} %fusion.42, pred[384,384]{1,0:T(8,128)(4,1)S(1)} %subtract_compare_fusion, f32[384,24,128]{2,1,0:T(8,128)S(1)} %bitcast.126), kind=kOutput, calls=%fused_computation.8 | convolution fusion | flops 5439356928 | bytes 23740416 | tf_op jit(solution)/shard_map/hij,bjhc->bihc/dot_general | solution.py:71
  345.3 9.6 %fusion.15 = (bf16[1,384,24,128]{1,3,2,0:T(8,128)(2,1)}, bf16[1,384,24,128]{1,3,2,0:T(8,128)(2,1)}) fusion(f32[1,384,24,128]{1,3,2,0:T(8,128)} %copy.111, f32[1,384,24,128]{1,3,2,0:T(8,128)} %copy.107, f32[24,128,384]{2,1,0:T(8,128)} %fusion.4, f32[24,16]{1,0:T(8,128)S(1)} %get-tuple-element.215, f32[24,16]{1,0:T(8,128)S(1)} %get-tuple-element.225, ...), kind=kOutput, calls=%fused_computation.23 | convolution fusion | flops 232734720 | bytes 19075584 | tf_op jit(solution)/shard_map/hmi,bhmc->bihc/dot_general | solution.py:90
  354.9 3.1 copy.108
  358.0 2.4 convert_element_type.134
  360.4 34.3 %all_to_all.118 = bf16[2,192,3072]{2,1,0:T(8,128)(2,1)S(1)} all-to-all(bf16[2,192,3072]{2,1,0:T(8,128)(2,1)} %convert_element_type.134), channel_id=1, replica_groups=mesh['ctx'=64,'head'=2] {'head'}, dimensions={0} | all-to-all | bytes 4718592 | tf_op jit(solution)/shard_map/all_to_all | solution.py:163
  394.7 1.6 copy.139
  396.3 3.1 copy.112
  399.4 2.4 convert_element_type.139
  401.8 6.9 all_to_all.119
  408.7 1.6 copy.140
  410.4 256.6 %all-gather.3 = f32[64,24,16]{1,2,0:T(8,128)S(1)} all-gather(f32[1,24,16]{1,2,0:T(8,128)S(1)} %copy.125), channel_id=3, replica_groups=mesh['ctx'=64,'head'=2] {'ctx'}, dimensions={0}, use_global_device_ids=true | all-gather | bytes 99840 | tf_op jit(solution)/shard_map/all_gather | solution.py:169
  667.6 19.5 %fusion.2 = f32[24,128,384]{2,1,0:T(8,128)} fusion(f32[24,384,384]{2,1,0:T(8,128)} %fusion.42, pred[384,384]{1,0:T(8,128)(4,1)S(1)} %subtract_compare_fusion, f32[384,24,128]{2,1,0:T(8,128)} %bitcast.121), kind=kOutput, calls=%fused_computation.6 | convolution fusion | flops 5439356928 | bytes 23740416 | tf_op jit(solution)/shard_map/hij,bihc->bjhc/dot_general | solution.py:95
  687.2 112.8 %while.17 = (s32[]{:T(128)}, f32[24,16,128]{2,1,0:T(8,128)S(1)}, s32[]{:T(128)}, f32[64,24,16]{2,1,0:T(8,128)}, f32[64,24,16,128]{3,2,1,0:T(8,128)}, /*index=5*/s32[]{:T(128)}, s32[]{:T(128)}, s32[]{:T(128)}, s32[]{:T(128)}) while((s32[]{:T(128)}, f32[24,16,128]{2,1,0:T(8,128)S(1)}, s32[]{:T(128)}, f32[64,24,16]{2,1,0:T(8,128)}, ...), condition=%wide.region_3.4_spmd, body=%wide.region_2.3_spmd.sunk | while | flops 98310 | bytes 594587 | solution.py:25
  687.9 1.0 bitcast_add_fusion.6
  691.5 1.0 bitcast_add_fusion.6
  693.3 1.0 bitcast_add_fusion.6
  696.8 1.0 bitcast_add_fusion.6
  698.6 1.0 bitcast_add_fusion.6
  700.4 1.0 bitcast_add_fusion.6
  704.0 1.0 bitcast_add_fusion.6
  705.8 1.0 bitcast_add_fusion.6
  707.6 1.0 bitcast_add_fusion.6
  711.2 1.0 bitcast_add_fusion.6
  713.0 1.0 bitcast_add_fusion.6
  716.5 1.0 bitcast_add_fusion.6
  800.0 9.6 %fusion.13 = (bf16[1,384,24,128]{1,3,2,0:T(8,128)(2,1)}, bf16[1,384,24,128]{1,3,2,0:T(8,128)(2,1)}) fusion(f32[1,384,24,128]{1,3,2,0:T(8,128)} %copy.120, f32[1,384,24,128]{1,3,2,0:T(8,128)} %copy.117, f32[24,128,384]{2,1,0:T(8,128)} %fusion.2, f32[24,16]{1,0:T(8,128)S(1)} %get-tuple-element.215, f32[384]{0:T(512)S(1)} %iota_subtract_fusion, ...), kind=kOutput, calls=%fused_computation.19 | convolution fusion | flops 232734720 | bytes 19077120 | tf_op jit(solution)/shard_map/hmj,bhmc->bjhc/dot_general | solution.py:105
  809.6 3.1 copy.118
  812.7 2.4 convert_element_type.146
  815.1 35.0 %all_to_all.120 = bf16[2,192,3072]{2,1,0:T(8,128)(2,1)S(1)} all-to-all(bf16[2,192,3072]{2,1,0:T(8,128)(2,1)} %convert_element_type.146), channel_id=1, replica_groups=mesh['ctx'=64,'head'=2] {'head'}, dimensions={0} | all-to-all | bytes 4718592 | tf_op jit(solution)/shard_map/all_to_all | solution.py:165
  850.1 1.6 copy.141
  851.7 3.1 copy.121
  854.8 2.4 convert_element_type.151
  857.2 6.8 all_to_all.121
  864.1 1.6 copy.142
  (152 shorter events, 103.4 us)
Async XLA Ops:
  7.2 8.5 copy-start.3
  7.2 8.5 copy-start.4
  10.4 8.6 all-to-all-start.2
  15.6 200.3 %all-gather.7.cloned.1.call-start = ((), (), s32[]{:S(2)}) async-start(), calls=%async_computation.8 | async-start | bytes 12779520 | tf_op jit(solution)/shard_map/all_gather | solution.py:16
  25.6 1.4 copy-start.1
  28.0 2.1 copy-start
  37.6 8.5 all-to-all-start.4
  42.8 644.3 %all-gather.9.cloned.1.call-start = ((), (), s32[]{:S(2)}) async-start(), calls=%async_computation.9 | async-start | bytes 12779520 | tf_op jit(solution)/shard_map/all_gather | solution.py:16
  52.7 3.4 copy-start.2
  293.9 27.9 %slice-start = ((s8[4718592]{0:T(1024)(128)(4,1)}), s8[4194304]{0:T(1024)(128)(4,1)S(1)}, s32[]{:S(2)}) async-start(s8[4718592]{0:T(1024)(128)(4,1)} %bitcast.124), calls=%async_computation.10 | async-start | bytes 8388608
  307.4 14.4 %slice-start.1 = ((s8[4718592]{0:T(1024)(128)(4,1)}), s8[524288]{0:T(1024)(128)(4,1)S(1)}, s32[]{:S(2)}) async-start(s8[4718592]{0:T(1024)(128)(4,1)} %bitcast.124), calls=%async_computation.11 | async-start | bytes 1048576
Sparse Core Ops, SparseCore 0:
  34.5 94.2 all-gather.6
  233.9 224.8 all-gather.8
